TPU v7x, 32 devices: a whole 2x2x4 slice. The times are simulated.
32 devices in a mesh: groups: 2 (over y), feat: 4 (over z), tok: 2 (over x), rep: 2 (over core).
Axes of the slice: x: 2, y: 2, z: 4, core: 2. Of those that a mesh axis runs over, the one named last changes fastest.
Arguments:
- tokens: bfloat16 [448, 8192], P(('groups', 'tok', 'rep'), 'feat'), parts along dimension 0, may hold values from -6 to 6
- gate_weight: bfloat16 [8192, 14336], P('feat', ('tok', 'rep')), may hold values from -0.09375 to 0.09375
- up_weight: bfloat16 [8192, 14336], P('feat', ('tok', 'rep')), may hold values from -0.09375 to 0.09375
- down_weight: bfloat16 [14336, 8192], P(('tok', 'rep'), 'feat'), may hold values from -0.0625 to 0.0625
- gate_mask: int32 [64, 112], P('feat', ('tok', 'rep')), may hold values 0 or 1
- up_mask: int32 [64, 112], P('feat', ('tok', 'rep')), may hold values 0 or 1
- down_mask: int32 [112, 64], P(('tok', 'rep'), 'feat'), may hold values 0 or 1
Outputs:
- mixed: bfloat16 [448, 8192], P(('groups', 'tok', 'rep'), 'feat'), parts along dimension 0
There are 2 independent parts, one for each index of `groups`. A program takes and returns all parts, laid end to end along the dimension named above; an argument that names none is the same for every part. Nothing has to cross between parts.
Inputs may be any that keep to these rules, and one draw needn't show every extreme that they name: `gate_mask`: entries are 0 or 1; 1 keeps the block. `up_mask`: entries are 0 or 1; 1 keeps the block. `down_mask`: entries are 0 or 1; 1 keeps the block.
All inputs are finite; a program needn't handle non-finite values.
Results may differ from a plain program's by a relative error of at most 0.02.
Values may be sent and summed in bfloat16 or wider, within the bound.
A program may use at most 192 MiB of HBM per device.

v0:
```python
import functools

import jax
import jax.numpy as jnp
from jax import lax
from jax.experimental import pallas as pl
from jax.experimental.pallas import tpu as pltpu
from jax.sharding import PartitionSpec as P

BLOCK = 128
HOP = 2
BACK = 2
LEAD = 2
DELAY = 3
EARLY = 2
MESH = pl.DeviceIdType.MESH


def kernel(nf, nx, nr, tokens, gate_w, up_w, down_w, gate_m, up_m, down_m, out,
           arrived, tok, wgu, wd, sums, part, taken, hid, acc, leaving, coming,
           tok_send, tok_recv, own_sem, g_sem, u_sem, d_sem, part_send, part_recv,
           hid_send, hid_recv, out_send, out_recv):
    z, x, r = lax.axis_index("feat"), lax.axis_index("tok"), lax.axis_index("rep")
    rows = arrived.shape[1]
    feats = tok.shape[2]
    chunks = wgu.shape[0]
    width = wd.shape[1]
    up_chunks, down_chunks = (chunks + 1) // 2, chunks // 2
    early = min(EARLY, down_chunks)
    peers = [(g, q) for g in range(nx) for q in range(nr)]

    def chip(g):
        return lax.rem(x + 1 + g, nx)

    barrier = pltpu.get_barrier_semaphore()
    for g in range(nx - 1):
        for q in range(nr):
            pl.semaphore_signal(barrier, inc=1, device_id={"tok": chip(g), "rep": q}, device_id_type=MESH)
    for step in range(1, nr):
        pl.semaphore_signal(barrier, inc=1, device_id={"rep": lax.rem(r + step, nr)}, device_id_type=MESH)

    @pl.when(z > 0)
    def _():
        pl.semaphore_signal(barrier, inc=1, device_id={"feat": z - 1}, device_id_type=MESH)

    @pl.when(z < nf - 1)
    def _():
        pl.semaphore_signal(barrier, inc=1, device_id={"feat": z + 1}, device_id_type=MESH)

    def gate_copy(j):
        cols = pl.ds(pl.multiple_of(j * width, width), width)
        return pltpu.make_async_copy(gate_w.at[:, cols], wgu.at[j, :, pl.ds(0, width)], g_sem.at[j])

    def up_copy(j):
        cols = pl.ds(pl.multiple_of(j * width, width), width)
        return pltpu.make_async_copy(up_w.at[:, cols], wgu.at[j, :, pl.ds(width, width)], u_sem.at[j])

    def down_copy(j):
        at = pl.ds(pl.multiple_of(j * width, width), width)
        return pltpu.make_async_copy(down_w.at[at, :], wd.at[j], d_sem.at[j])

    own_copy = pltpu.make_async_copy(tokens, arrived.at[(nx - 1) * nr + r], own_sem)
    own_copy.start()

    def fetch(c, make):
        make(c).start()
        if up_chunks == down_chunks:
            make(up_chunks + c).start()
        else:
            @pl.when(c < down_chunks)
            def _():
                make(up_chunks + c).start()

    lead = min(LEAD, up_chunks)
    for c in range(lead):
        fetch(jnp.int32(c), gate_copy)
        fetch(jnp.int32(c), up_copy)
    acc[...] = jnp.zeros_like(acc)

    ends = (z == 0).astype(jnp.int32) + (z == nf - 1).astype(jnp.int32)
    pl.semaphore_wait(barrier, nx * nr + 1 - ends)

    def near_copy(step):
        return pltpu.make_async_remote_copy(
            src_ref=tokens, dst_ref=arrived.at[(nx - 1) * nr + r],
            send_sem=tok_send.at[(nx - 1) * nr + step], recv_sem=tok_recv.at[(nx - 1) * nr + r],
            device_id={"rep": lax.rem(r + step, nr)}, device_id_type=MESH)

    def far_copy(g, q):
        slot = (nx - 2 - g) * nr + r
        return pltpu.make_async_remote_copy(
            src_ref=tokens, dst_ref=arrived.at[slot],
            send_sem=tok_send.at[g * nr + q], recv_sem=tok_recv.at[slot],
            device_id={"tok": chip(g), "rep": q}, device_id_type=MESH)

    def landed(slot):
        pltpu.make_async_remote_copy(
            src_ref=tokens, dst_ref=arrived.at[slot],
            send_sem=tok_send.at[0], recv_sem=tok_recv.at[slot],
            device_id={"rep": lax.rem(r + 1, nr)}, device_id_type=MESH).wait_recv()

    for step in range(1, nr):
        near_copy(step).start()
    for g in range(nx - 1):
        for q in range(nr):
            far_copy(g, q).start()
    own_copy.wait()
    for step in range(1, nr):
        landed((nx - 1) * nr + lax.rem(r + step, nr))
    for q in range(nr):
        tok[nx - 1, q * rows:(q + 1) * rows, :] = arrived[(nx - 1) * nr + q]

    def place(d):
        p = jnp.where(d == 0, z, nf - 1 - z)
        count = up_chunks if up_chunks == down_chunks else jnp.where(d == 0, up_chunks, down_chunks)
        return p, count, nx * count

    def unit(u, d, count):
        mine = (u < early) | (u >= early + (nx - 1) * count)
        other = jnp.maximum(u - early, 0)
        group = jnp.where(mine, nx - 1, other // count)
        c = jnp.where(u < early, u, jnp.where(mine, u - (nx - 1) * count, other % count))
        first = (u < early) | ((u >= 2 * early) & (u < early + count))
        return group, d * up_chunks + c, first

    def ahead(d):
        return z + 1 - 2 * d

    def behind(d):
        return z - 1 + 2 * d

    def part_copy(d, u):
        return pltpu.make_async_remote_copy(
            src_ref=part.at[d, u], dst_ref=taken.at[d, u],
            send_sem=part_send.at[d, u], recv_sem=part_recv.at[d, u],
            device_id={"feat": ahead(d)}, device_id_type=MESH)

    def hid_copy(d, u):
        return pltpu.make_async_remote_copy(
            src_ref=hid.at[d, u], dst_ref=hid.at[d, u],
            send_sem=hid_send.at[d, u], recv_sem=hid_recv.at[d, u],
            device_id={"feat": behind(d)}, device_id_type=MESH)

    def splat(scalar, shape):
        return jnp.full(shape, scalar.astype(jnp.float32)).astype(jnp.bfloat16)

    def first_half(i, d):
        p, count, units = place(d)
        u = i - HOP * p

        @pl.when((u >= 0) & (u < units))
        def _():
            group, j, first = unit(u, d, count)

            @pl.when(first)
            def _():
                gate_copy(j).wait()
                up_copy(j).wait()

            total = None
            deep = 2 * BLOCK if feats % (2 * BLOCK) == 0 else BLOCK
            for lo in range(0, feats, deep):
                tall = []
                for b in range(lo // BLOCK, (lo + deep) // BLOCK):
                    wide = []
                    for n in range(2 * width // BLOCK):
                        mask = gate_m if n < width // BLOCK else up_m
                        keep = mask[b, j * (width // BLOCK) + n % (width // BLOCK)]
                        wide.append(wgu[j, b * BLOCK:(b + 1) * BLOCK, n * BLOCK:(n + 1) * BLOCK] * splat(keep, (BLOCK, BLOCK)))
                    tall.append(jnp.concatenate(wide, axis=1))
                product = jnp.dot(tok[group, :, lo:lo + deep], jnp.concatenate(tall, axis=0),
                                  preferred_element_type=jnp.float32)
                total = product if total is None else total + product
            sums[...] = total

            @pl.when(p > 0)
            def _():
                part_copy(d, u).wait_recv()
                sums[...] += taken[d, u].astype(jnp.float32)

            @pl.when(p < nf - 1)
            def _():
                part[d, u] = sums[...].astype(jnp.bfloat16)
                part_copy(d, u).start()

            @pl.when(p == nf - 1)
            def _():
                gate, up = sums[:, :width], sums[:, width:]
                hid[d, u] = (gate / (1.0 + jnp.exp(-gate)) * up).astype(jnp.bfloat16)

    def second_half(i, d):
        p, count, units = place(d)
        h = i - HOP * (nf - 1) - DELAY - BACK * (nf - 1 - p)

        @pl.when((h >= 0) & (h < units))
        def _():
            group, j, first = unit(h, d, count)

            @pl.when(p < nf - 1)
            def _():
                hid_copy(d, h).wait_recv()

            @pl.when(p > 0)
            def _():
                hid_copy(d, h).start()

            @pl.when(first)
            def _():
                down_copy(j).wait()

            for n in range(wd.shape[2] // BLOCK // 2):
                cols = slice(2 * n * BLOCK, 2 * (n + 1) * BLOCK)
                tall = []
                for b in range(width // BLOCK):
                    wide = []
                    for m in (2 * n, 2 * n + 1):
                        keep = down_m[m, j * (width // BLOCK) + b]
                        wide.append(wd[j, b * BLOCK:(b + 1) * BLOCK, m * BLOCK:(m + 1) * BLOCK] * splat(keep, (BLOCK, BLOCK)))
                    tall.append(jnp.concatenate(wide, axis=1))
                acc[group, :, cols] += jnp.dot(hid[d, h], jnp.concatenate(tall, axis=0),
                                               preferred_element_type=jnp.float32)

    def out_copy(g, q):
        slot = g * nr + r
        return pltpu.make_async_remote_copy(
            src_ref=leaving.at[g * nr + q], dst_ref=coming.at[slot],
            send_sem=out_send.at[g * nr + q], recv_sem=out_recv.at[slot],
            device_id={"tok": chip(g), "rep": q}, device_id_type=MESH)

    def last_copy(step):
        return pltpu.make_async_remote_copy(
            src_ref=leaving.at[(nx - 1) * nr + step], dst_ref=coming.at[(nx - 1) * nr + r],
            send_sem=out_send.at[(nx - 1) * nr + step], recv_sem=out_recv.at[(nx - 1) * nr + r],
            device_id={"rep": lax.rem(r + step, nr)}, device_id_type=MESH)

    starts = HOP * jnp.minimum(z, nf - 1 - z) + early

    @pl.loop(0, nx * up_chunks + (HOP + BACK) * (nf - 1) + DELAY)
    def _(i):
        @pl.when(i == starts)
        def _():
            for g in range(nx - 1):
                for q in range(nr):
                    landed(g * nr + q)
                    tok[g, q * rows:(q + 1) * rows, :] = arrived[g * nr + q]

        @pl.when(i + lead < up_chunks)
        def _():
            fetch(i + lead, gate_copy)
            fetch(i + lead, up_copy)

        @pl.when(i < up_chunks)
        def _():
            fetch(i, down_copy)

        @pl.loop(0, 2)
        def _(d):
            first_half(i, d)

        @pl.loop(0, 2)
        def _(d):
            second_half(i, d)

        for g in range(nx - 1):
            ends = [early + (g + 1) * count - 1 + HOP * (nf - 1) + DELAY + BACK * (nf - 1 - p)
                    for count, p in ((up_chunks, z), (down_chunks, nf - 1 - z))]

            @pl.when(i == jnp.maximum(*ends))
            def _():
                for q in range(nr):
                    leaving[g * nr + q] = acc[g, q * rows:(q + 1) * rows, :].astype(jnp.bfloat16)
                    out_copy(g, q).start()

    for step in range(1, nr):
        at = pl.ds(pl.multiple_of(lax.rem(r + step, nr) * rows, 8), rows)
        leaving[(nx - 1) * nr + step] = acc[nx - 1, at, :].astype(jnp.bfloat16)
        last_copy(step).start()
    final = acc[nx - 1, pl.ds(pl.multiple_of(r * rows, 8), rows), :]

    def summed(slot):
        pltpu.make_async_remote_copy(
            src_ref=leaving.at[0], dst_ref=coming.at[slot],
            send_sem=out_send.at[0], recv_sem=out_recv.at[slot],
            device_id={"rep": lax.rem(r + 1, nr)}, device_id_type=MESH).wait_recv()
        return coming[slot].astype(jnp.float32)

    for slot in range((nx - 1) * nr):
        final += summed(slot)
    for step in range(1, nr):
        final += summed((nx - 1) * nr + lax.rem(r + step, nr))
    out[...] = final.astype(out.dtype)

    for step in range(1, nr):
        near_copy(step).wait_send()
        last_copy(step).wait_send()
    for g in range(nx - 1):
        for q in range(nr):
            far_copy(g, q).wait_send()
            out_copy(g, q).wait_send()

    @pl.loop(0, 2)
    def _(d):
        p, count, units = place(d)

        @pl.loop(0, nx * up_chunks)
        def _(u):
            @pl.when((u < units) & (p < nf - 1))
            def _():
                part_copy(d, u).wait_send()

            @pl.when((u < units) & (p > 0))
            def _():
                hid_copy(d, u).wait_send()


def solution(mesh):
    nf, nx, nr = mesh.shape["feat"], mesh.shape["tok"], mesh.shape["rep"]

    def shards(tokens, gate_weight, up_weight, down_weight, gate_mask, up_mask, down_mask):
        rows, feats = tokens.shape
        hidden = gate_weight.shape[1]
        width = 2 * BLOCK if hidden % (4 * BLOCK) == 0 else BLOCK
        chunks = hidden // width
        units = nx * ((chunks + 1) // 2)
        high = nr * rows
        bf16, f32 = jnp.bfloat16, jnp.float32
        dma = pltpu.SemaphoreType.DMA
        hbm, smem = pl.BlockSpec(memory_space=pl.ANY), pl.BlockSpec(memory_space=pltpu.SMEM)
        return pl.pallas_call(
            functools.partial(kernel, nf, nx, nr),
            out_shape=jax.ShapeDtypeStruct((rows, feats), bf16),
            in_specs=[hbm] * 4 + [smem] * 3,
            out_specs=pl.BlockSpec(memory_space=pltpu.VMEM),
            scratch_shapes=[
                pltpu.VMEM((nx * nr, rows, feats), bf16),
                pltpu.VMEM((nx, high, feats), bf16),
                pltpu.VMEM((chunks, feats, 2 * width), bf16),
                pltpu.VMEM((chunks, width, feats), bf16),
                pltpu.VMEM((high, 2 * width), f32),
                pltpu.VMEM((2, units, high, 2 * width), bf16),
                pltpu.VMEM((2, units, high, 2 * width), bf16),
                pltpu.VMEM((2, units, high, width), bf16),
                pltpu.VMEM((nx, high, feats), f32),
                pltpu.VMEM((nx * nr, rows, feats), bf16),
                pltpu.VMEM((nx * nr, rows, feats), bf16),
                dma((nx * nr,)), dma((nx * nr,)), dma(()),
                dma((chunks,)), dma((chunks,)), dma((chunks,)),
                dma((2, units)), dma((2, units)), dma((2, units)), dma((2, units)),
                dma((nx * nr,)), dma((nx * nr,)),
            ],
            compiler_params=pltpu.CompilerParams(
                collective_id=0, has_side_effects=True, vmem_limit_bytes=63 * 1024 * 1024),
        )(tokens, gate_weight, up_weight, down_weight, gate_mask, up_mask, down_mask.T)

    return jax.shard_map(
        shards,
        mesh=mesh,
        in_specs=(
            P(("groups", "tok", "rep"), "feat"),
            P("feat", ("tok", "rep")),
            P("feat", ("tok", "rep")),
            P(("tok", "rep"), "feat"),
            P("feat", ("tok", "rep")),
            P("feat", ("tok", "rep")),
            P(("tok", "rep"), "feat"),
        ),
        out_specs=P(("groups", "tok", "rep"), "feat"),
        check_vma=False,
    )
```

profile of v0, /device:TPU:0, one launch (start us, length us, event | category | flops | bytes accessed | tf_op | source)
XLA Modules:
  0.0 81.5 jit_solution(1278977928779554367)
XLA Ops:
  0.0 79.9 %shard_map.73 = bf16[56,2048]{1,0:T(8,128)(2,1)} custom-call(bf16[56,2048]{1,0:T(8,128)(2,1)} %tokens.1, bf16[2048,3584]{1,0:T(8,128)(2,1)} %gate_w.1, bf16[2048,3584]{1,0:T(8,128)(2,1)} %up_w.1, bf16[3584,2048]{1,0:T(8,128)(2,1)} %down_w.1, s32[16,28]{1,0:T(8,128)} %gate_m.1, s32[16,28]{1,0:T(8,128)} %up_m.1, s32[16,28]{1,0:T(8,128)} %bitcast.1), custom_call_target="tpu_custom_call" | custom-call | tf_op jit(solution)/shard_map/pallas_call | solution.py:329
  79.9 1.6 %copy.9 = bf16[56,2048]{1,0:T(8,128)(2,1)} copy(bf16[56,2048]{1,0:T(8,128)(2,1)} %shard_map.73) | data formatting | bytes 458752
where the time goes:
time: 82.4 us; the launch traced here: 81.5 us
  Pallas kernels  79.9 us (97%)
  local copies, waits for them, and re-layouts  1.64 us (2%)
    pallas_call x1, Pallas kernels, shards(): pl.pallas_call(functools.partial(kernel, nf, nx, nr), out_shape=jax.Shape...  79.9 us

commit v1 on v0

--- a/solution.py
+++ b/solution.py
@@ -8,11 +8,11 @@
 from jax.sharding import PartitionSpec as P
 
 BLOCK = 128
-HOP = 2
-BACK = 2
+HOP = 3
+BACK = 3
 LEAD = 2
-DELAY = 3
-EARLY = 2
+SLACK = 2
+EARLY = 5
 MESH = pl.DeviceIdType.MESH
 
 
@@ -62,19 +62,12 @@
     own_copy = pltpu.make_async_copy(tokens, arrived.at[(nx - 1) * nr + r], own_sem)
     own_copy.start()
 
-    def fetch(c, make):
-        make(c).start()
-        if up_chunks == down_chunks:
-            make(up_chunks + c).start()
-        else:
-            @pl.when(c < down_chunks)
-            def _():
-                make(up_chunks + c).start()
-
-    lead = min(LEAD, up_chunks)
+    lead = min(LEAD, down_chunks)
     for c in range(lead):
-        fetch(jnp.int32(c), gate_copy)
-        fetch(jnp.int32(c), up_copy)
+        for e in range(2):
+            j = jnp.where((z <= nf - 1 - z) == (e == 0), 0, up_chunks) + c
+            gate_copy(j).start()
+            up_copy(j).start()
     acc[...] = jnp.zeros_like(acc)
 
     ends = (z == 0).astype(jnp.int32) + (z == nf - 1).astype(jnp.int32)
@@ -129,10 +122,15 @@
     def behind(d):
         return z - 1 + 2 * d
 
-    def part_copy(d, u):
-        return pltpu.make_async_remote_copy(
-            src_ref=part.at[d, u], dst_ref=taken.at[d, u],
-            send_sem=part_send.at[d, u], recv_sem=part_recv.at[d, u],
+    def hidden_unit(h, count):
+        others = (nx - 1) * count
+        c = h - others
+        return jnp.where(c < 0, early + h, jnp.where(c < early, c, h))
+
+    def part_copy(d, u, m):
+        return pltpu.make_async_remote_copy(
+            src_ref=part.at[d, u, m], dst_ref=taken.at[d, u, m],
+            send_sem=part_send.at[d, u, m], recv_sem=part_recv.at[d, u, m],
             device_id={"feat": ahead(d)}, device_id_type=MESH)
 
     def hid_copy(d, u):
@@ -144,13 +142,28 @@
     def splat(scalar, shape):
         return jnp.full(shape, scalar.astype(jnp.float32)).astype(jnp.bfloat16)
 
-    def first_half(i, d):
+    others = (nx - 1) * up_chunks
+    begin = HOP * (nf - 1) + max(nr * (early + others) - others, (nr - 1) * nx * up_chunks) + SLACK
+
+    def multiply(k, d):
         p, count, units = place(d)
-        u = i - HOP * p
-
-        @pl.when((u >= 0) & (u < units))
+        t = k - HOP * p + nr
+        u = t // nr
+
+        @pl.when((t >= 0) & (u < units) & (t % nr == 0))
         def _():
             group, j, first = unit(u, d, count)
+
+            @pl.when(u + lead < count)
+            def _():
+                gate_copy(d * up_chunks + u + lead).start()
+                up_copy(d * up_chunks + u + lead).start()
+
+            below = u - (count - lead if nx > 1 else 0)
+
+            @pl.when((below >= 0) & (below < count))
+            def _():
+                down_copy(d * up_chunks + below).start()
 
             @pl.when(first)
             def _():
@@ -171,40 +184,52 @@
                 product = jnp.dot(tok[group, :, lo:lo + deep], jnp.concatenate(tall, axis=0),
                                   preferred_element_type=jnp.float32)
                 total = product if total is None else total + product
-            sums[...] = total
+            for m in range(nr):
+                sums[d, u % 2, m] = total[m * rows:(m + 1) * rows, :]
+
+    def reduce(k, d):
+        p, count, units = place(d)
+        t = k - HOP * p
+        u, m = t // nr, t % nr
+
+        @pl.when((t >= 0) & (u < units))
+        def _():
+            here = sums.at[d, u % 2, m]
 
             @pl.when(p > 0)
             def _():
-                part_copy(d, u).wait_recv()
-                sums[...] += taken[d, u].astype(jnp.float32)
+                part_copy(d, u, m).wait_recv()
+                here[...] += taken[d, u, m].astype(jnp.float32)
 
             @pl.when(p < nf - 1)
             def _():
-                part[d, u] = sums[...].astype(jnp.bfloat16)
-                part_copy(d, u).start()
-
-            @pl.when(p == nf - 1)
-            def _():
-                gate, up = sums[:, :width], sums[:, width:]
-                hid[d, u] = (gate / (1.0 + jnp.exp(-gate)) * up).astype(jnp.bfloat16)
-
-    def second_half(i, d):
+                part[d, u, m] = here[...].astype(jnp.bfloat16)
+                part_copy(d, u, m).start()
+
+            for s in range(nr):
+                @pl.when((p == nf - 1) & (m == s))
+                def _():
+                    gate, up = here[:, :width], here[:, width:]
+                    hid[d, u, s * rows:(s + 1) * rows, :] = (gate / (1.0 + jnp.exp(-gate)) * up).astype(jnp.bfloat16)
+
+    def spread(k, d):
         p, count, units = place(d)
-        h = i - HOP * (nf - 1) - DELAY - BACK * (nf - 1 - p)
+        h = k - begin - BACK * (nf - 1 - p)
 
         @pl.when((h >= 0) & (h < units))
         def _():
-            group, j, first = unit(h, d, count)
+            u = hidden_unit(h, count)
+            group, j, _ = unit(u, d, count)
 
             @pl.when(p < nf - 1)
             def _():
-                hid_copy(d, h).wait_recv()
+                hid_copy(d, u).wait_recv()
 
             @pl.when(p > 0)
             def _():
-                hid_copy(d, h).start()
-
-            @pl.when(first)
+                hid_copy(d, u).start()
+
+            @pl.when(h < count)
             def _():
                 down_copy(j).wait()
 
@@ -217,7 +242,7 @@
                         keep = down_m[m, j * (width // BLOCK) + b]
                         wide.append(wd[j, b * BLOCK:(b + 1) * BLOCK, m * BLOCK:(m + 1) * BLOCK] * splat(keep, (BLOCK, BLOCK)))
                     tall.append(jnp.concatenate(wide, axis=1))
-                acc[group, :, cols] += jnp.dot(hid[d, h], jnp.concatenate(tall, axis=0),
+                acc[group, :, cols] += jnp.dot(hid[d, u], jnp.concatenate(tall, axis=0),
                                                preferred_element_type=jnp.float32)
 
     def out_copy(g, q):
@@ -233,39 +258,35 @@
             send_sem=out_send.at[(nx - 1) * nr + step], recv_sem=out_recv.at[(nx - 1) * nr + r],
             device_id={"rep": lax.rem(r + step, nr)}, device_id_type=MESH)
 
-    starts = HOP * jnp.minimum(z, nf - 1 - z) + early
-
-    @pl.loop(0, nx * up_chunks + (HOP + BACK) * (nf - 1) + DELAY)
-    def _(i):
-        @pl.when(i == starts)
+    starts = HOP * jnp.minimum(z, nf - 1 - z) + nr * early - nr
+    flip = (z > nf - 1 - z).astype(jnp.int32)
+
+    @pl.loop(-nr, begin + BACK * (nf - 1) + nx * up_chunks)
+    def _(k):
+        @pl.loop(0, 2)
+        def _(e):
+            reduce(k, (e + flip) % 2)
+
+        @pl.when(k == starts)
         def _():
             for g in range(nx - 1):
                 for q in range(nr):
                     landed(g * nr + q)
                     tok[g, q * rows:(q + 1) * rows, :] = arrived[g * nr + q]
 
-        @pl.when(i + lead < up_chunks)
-        def _():
-            fetch(i + lead, gate_copy)
-            fetch(i + lead, up_copy)
-
-        @pl.when(i < up_chunks)
-        def _():
-            fetch(i, down_copy)
-
         @pl.loop(0, 2)
-        def _(d):
-            first_half(i, d)
+        def _(e):
+            multiply(k, (e + flip) % 2)
 
         @pl.loop(0, 2)
-        def _(d):
-            second_half(i, d)
+        def _(e):
+            spread(k, (e + flip) % 2)
 
         for g in range(nx - 1):
-            ends = [early + (g + 1) * count - 1 + HOP * (nf - 1) + DELAY + BACK * (nf - 1 - p)
+            ends = [begin + BACK * (nf - 1 - p) + (g + 1) * count - 1
                     for count, p in ((up_chunks, z), (down_chunks, nf - 1 - z))]
 
-            @pl.when(i == jnp.maximum(*ends))
+            @pl.when(k == jnp.maximum(*ends))
             def _():
                 for q in range(nr):
                     leaving[g * nr + q] = acc[g, q * rows:(q + 1) * rows, :].astype(jnp.bfloat16)
@@ -306,7 +327,8 @@
         def _(u):
             @pl.when((u < units) & (p < nf - 1))
             def _():
-                part_copy(d, u).wait_send()
+                for m in range(nr):
+                    part_copy(d, u, m).wait_send()
 
             @pl.when((u < units) & (p > 0))
             def _():
@@ -336,16 +358,16 @@
                 pltpu.VMEM((nx, high, feats), bf16),
                 pltpu.VMEM((chunks, feats, 2 * width), bf16),
                 pltpu.VMEM((chunks, width, feats), bf16),
-                pltpu.VMEM((high, 2 * width), f32),
-                pltpu.VMEM((2, units, high, 2 * width), bf16),
-                pltpu.VMEM((2, units, high, 2 * width), bf16),
+                pltpu.VMEM((2, 2, nr, rows, 2 * width), f32),
+                pltpu.VMEM((2, units, nr, rows, 2 * width), bf16),
+                pltpu.VMEM((2, units, nr, rows, 2 * width), bf16),
                 pltpu.VMEM((2, units, high, width), bf16),
                 pltpu.VMEM((nx, high, feats), f32),
                 pltpu.VMEM((nx * nr, rows, feats), bf16),
                 pltpu.VMEM((nx * nr, rows, feats), bf16),
                 dma((nx * nr,)), dma((nx * nr,)), dma(()),
                 dma((chunks,)), dma((chunks,)), dma((chunks,)),
-                dma((2, units)), dma((2, units)), dma((2, units)), dma((2, units)),
+                dma((2, units, nr)), dma((2, units, nr)), dma((2, units)), dma((2, units)),
                 dma((nx * nr,)), dma((nx * nr,)),
             ],
             compiler_params=pltpu.CompilerParams(

time: 82.4 us -> 76.3 us (0.926)
  Pallas kernels: 79.9 us -> 74.4 us
    pallas_call x1, Pallas kernels: 79.9 us -> 74.4 us  [shards(): pl.pallas_call(functools.partial(kernel, nf, nx, nr), out_shape=jax.Shape...]
where the time goes in v1:
time: 76.3 us; the launch traced here: 76.1 us
  Pallas kernels  74.4 us (98%)
  local copies, waits for them, and re-layouts  1.64 us (2%)
    pallas_call x1, Pallas kernels, shards(): pl.pallas_call(functools.partial(kernel, nf, nx, nr), out_shape=jax.Shape...  74.4 us
    unnamed x1, local copies, waits for them, and re-layouts  1.64 us

profile of v1, /device:TPU:0, one launch (start us, length us, event | category | flops | bytes accessed | tf_op | source)
XLA Modules:
  0.0 76.1 jit_solution(9340994647703489957)
XLA Ops:
  0.0 74.4 %shard_map.73 = bf16[56,2048]{1,0:T(8,128)(2,1)} custom-call(bf16[56,2048]{1,0:T(8,128)(2,1)} %tokens.1, bf16[2048,3584]{1,0:T(8,128)(2,1)} %gate_w.1, bf16[2048,3584]{1,0:T(8,128)(2,1)} %up_w.1, bf16[3584,2048]{1,0:T(8,128)(2,1)} %down_w.1, s32[16,28]{1,0:T(8,128)} %gate_m.1, s32[16,28]{1,0:T(8,128)} %up_m.1, s32[16,28]{1,0:T(8,128)} %bitcast.1), custom_call_target="tpu_custom_call" | custom-call | tf_op jit(solution)/shard_map/pallas_call | solution.py:351
  74.5 1.6 %copy.9 = bf16[56,2048]{1,0:T(8,128)(2,1)} copy(bf16[56,2048]{1,0:T(8,128)(2,1)} %shard_map.73) | data formatting | bytes 458752

commit v2 on v1

--- a/solution.py
+++ b/solution.py
@@ -13,13 +13,15 @@
 LEAD = 2
 SLACK = 2
 EARLY = 5
+HEADS = 2
+PAUSE = 2
 MESH = pl.DeviceIdType.MESH
 
 
 def kernel(nf, nx, nr, tokens, gate_w, up_w, down_w, gate_m, up_m, down_m, out,
-           arrived, tok, wgu, wd, sums, part, taken, hid, acc, leaving, coming,
+           arrived, tok, wgu, wd, sums, part, taken, hid, acc, leaving, coming, shared, crossed,
            tok_send, tok_recv, own_sem, g_sem, u_sem, d_sem, part_send, part_recv,
-           hid_send, hid_recv, out_send, out_recv):
+           hid_send, hid_recv, out_send, out_recv, cross_send, cross_recv):
     z, x, r = lax.axis_index("feat"), lax.axis_index("tok"), lax.axis_index("rep")
     rows = arrived.shape[1]
     feats = tok.shape[2]
@@ -66,9 +68,53 @@
     for c in range(lead):
         for e in range(2):
             j = jnp.where((z <= nf - 1 - z) == (e == 0), 0, up_chunks) + c
-            gate_copy(j).start()
-            up_copy(j).start()
+            gate_copy(j).start(priority=1)
+            up_copy(j).start(priority=1)
     acc[...] = jnp.zeros_like(acc)
+
+    def splat(scalar, shape):
+        return jnp.full(shape, scalar.astype(jnp.float32)).astype(jnp.bfloat16)
+
+    def product(left, j):
+        total = None
+        deep = 2 * BLOCK if feats % (2 * BLOCK) == 0 else BLOCK
+        for lo in range(0, feats, deep):
+            tall = []
+            for b in range(lo // BLOCK, (lo + deep) // BLOCK):
+                wide = []
+                for n in range(2 * width // BLOCK):
+                    mask = gate_m if n < width // BLOCK else up_m
+                    keep = mask[b, j * (width // BLOCK) + n % (width // BLOCK)]
+                    wide.append(wgu[j, b * BLOCK:(b + 1) * BLOCK, n * BLOCK:(n + 1) * BLOCK] * splat(keep, (BLOCK, BLOCK)))
+                tall.append(jnp.concatenate(wide, axis=1))
+            piece = jnp.dot(left[:, lo:lo + deep], jnp.concatenate(tall, axis=0), preferred_element_type=jnp.float32)
+            total = piece if total is None else total + piece
+        return total
+
+    def ahead(d):
+        return z + 1 - 2 * d
+
+    def behind(d):
+        return z - 1 + 2 * d
+
+    def part_copy(d, u, m):
+        return pltpu.make_async_remote_copy(
+            src_ref=part.at[d, u, m], dst_ref=taken.at[d, u, m],
+            send_sem=part_send.at[d, u, m], recv_sem=part_recv.at[d, u, m],
+            device_id={"feat": ahead(d)}, device_id_type=MESH)
+
+    heads = min(HEADS, down_chunks, early) if nr == 2 and nf > 1 else 0
+    own_copy.wait()
+    side = (z > 0).astype(jnp.int32)
+
+    @pl.when((z == 0) | (z == nf - 1))
+    def _():
+        @pl.loop(0, heads)
+        def _(c):
+            j = side * up_chunks + c
+            gate_copy(j).wait()
+            up_copy(j).wait()
+            part[side, c, 0] = product(arrived[(nx - 1) * nr + r], j).astype(jnp.bfloat16)
 
     ends = (z == 0).astype(jnp.int32) + (z == nf - 1).astype(jnp.int32)
     pl.semaphore_wait(barrier, nx * nr + 1 - ends)
@@ -92,12 +138,17 @@
             send_sem=tok_send.at[0], recv_sem=tok_recv.at[slot],
             device_id={"rep": lax.rem(r + 1, nr)}, device_id_type=MESH).wait_recv()
 
+    @pl.when((z == 0) | (z == nf - 1))
+    def _():
+        @pl.loop(0, heads)
+        def _(c):
+            part_copy(side, c, 0).start()
+
     for step in range(1, nr):
         near_copy(step).start()
     for g in range(nx - 1):
         for q in range(nr):
             far_copy(g, q).start()
-    own_copy.wait()
     for step in range(1, nr):
         landed((nx - 1) * nr + lax.rem(r + step, nr))
     for q in range(nr):
@@ -116,31 +167,16 @@
         first = (u < early) | ((u >= 2 * early) & (u < early + count))
         return group, d * up_chunks + c, first
 
-    def ahead(d):
-        return z + 1 - 2 * d
-
-    def behind(d):
-        return z - 1 + 2 * d
-
     def hidden_unit(h, count):
         others = (nx - 1) * count
         c = h - others
         return jnp.where(c < 0, early + h, jnp.where(c < early, c, h))
 
-    def part_copy(d, u, m):
-        return pltpu.make_async_remote_copy(
-            src_ref=part.at[d, u, m], dst_ref=taken.at[d, u, m],
-            send_sem=part_send.at[d, u, m], recv_sem=part_recv.at[d, u, m],
-            device_id={"feat": ahead(d)}, device_id_type=MESH)
-
     def hid_copy(d, u):
         return pltpu.make_async_remote_copy(
             src_ref=hid.at[d, u], dst_ref=hid.at[d, u],
             send_sem=hid_send.at[d, u], recv_sem=hid_recv.at[d, u],
             device_id={"feat": behind(d)}, device_id_type=MESH)
-
-    def splat(scalar, shape):
-        return jnp.full(shape, scalar.astype(jnp.float32)).astype(jnp.bfloat16)
 
     others = (nx - 1) * up_chunks
     begin = HOP * (nf - 1) + max(nr * (early + others) - others, (nr - 1) * nx * up_chunks) + SLACK
@@ -156,34 +192,21 @@
 
             @pl.when(u + lead < count)
             def _():
-                gate_copy(d * up_chunks + u + lead).start()
-                up_copy(d * up_chunks + u + lead).start()
+                gate_copy(d * up_chunks + u + lead).start(priority=1)
+                up_copy(d * up_chunks + u + lead).start(priority=1)
 
             below = u - (count - lead if nx > 1 else 0)
 
             @pl.when((below >= 0) & (below < count))
             def _():
-                down_copy(d * up_chunks + below).start()
-
-            @pl.when(first)
+                down_copy(d * up_chunks + below).start(priority=1)
+
+            @pl.when(first & ((p > 0) | (u >= heads)))
             def _():
                 gate_copy(j).wait()
                 up_copy(j).wait()
 
-            total = None
-            deep = 2 * BLOCK if feats % (2 * BLOCK) == 0 else BLOCK
-            for lo in range(0, feats, deep):
-                tall = []
-                for b in range(lo // BLOCK, (lo + deep) // BLOCK):
-                    wide = []
-                    for n in range(2 * width // BLOCK):
-                        mask = gate_m if n < width // BLOCK else up_m
-                        keep = mask[b, j * (width // BLOCK) + n % (width // BLOCK)]
-                        wide.append(wgu[j, b * BLOCK:(b + 1) * BLOCK, n * BLOCK:(n + 1) * BLOCK] * splat(keep, (BLOCK, BLOCK)))
-                    tall.append(jnp.concatenate(wide, axis=1))
-                product = jnp.dot(tok[group, :, lo:lo + deep], jnp.concatenate(tall, axis=0),
-                                  preferred_element_type=jnp.float32)
-                total = product if total is None else total + product
+            total = product(tok[group], j)
             for m in range(nr):
                 sums[d, u % 2, m] = total[m * rows:(m + 1) * rows, :]
 
@@ -191,10 +214,13 @@
         p, count, units = place(d)
         t = k - HOP * p
         u, m = t // nr, t % nr
-
-        @pl.when((t >= 0) & (u < units))
+        if heads == 2:
+            u, m = jnp.where(t < 4, t % 2, u), jnp.where(t < 4, t // 2, m)
+        block = (r + m) % nr
+
+        @pl.when((t >= jnp.where(p == 0, heads, 0)) & (u < units))
         def _():
-            here = sums.at[d, u % 2, m]
+            here = sums.at[d, u % 2, block]
 
             @pl.when(p > 0)
             def _():
@@ -207,7 +233,7 @@
                 part_copy(d, u, m).start()
 
             for s in range(nr):
-                @pl.when((p == nf - 1) & (m == s))
+                @pl.when((p == nf - 1) & (block == s))
                 def _():
                     gate, up = here[:, :width], here[:, width:]
                     hid[d, u, s * rows:(s + 1) * rows, :] = (gate / (1.0 + jnp.exp(-gate)) * up).astype(jnp.bfloat16)
@@ -245,17 +271,31 @@
                 acc[group, :, cols] += jnp.dot(hid[d, u], jnp.concatenate(tall, axis=0),
                                                preferred_element_type=jnp.float32)
 
-    def out_copy(g, q):
-        slot = g * nr + r
-        return pltpu.make_async_remote_copy(
-            src_ref=leaving.at[g * nr + q], dst_ref=coming.at[slot],
-            send_sem=out_send.at[g * nr + q], recv_sem=out_recv.at[slot],
-            device_id={"tok": chip(g), "rep": q}, device_id_type=MESH)
+    def cross_copy(g, step):
+        return pltpu.make_async_remote_copy(
+            src_ref=shared.at[g, step], dst_ref=crossed.at[g, r],
+            send_sem=cross_send.at[g, step], recv_sem=cross_recv.at[g, r],
+            device_id={"rep": lax.rem(r + step, nr)}, device_id_type=MESH)
+
+    def crossing(g, q):
+        return pltpu.make_async_remote_copy(
+            src_ref=shared.at[g, 0], dst_ref=crossed.at[g, q],
+            send_sem=cross_send.at[g, 0], recv_sem=cross_recv.at[g, q],
+            device_id={"rep": lax.rem(r + 1, nr)}, device_id_type=MESH)
+
+    def out_copy(g):
+        return pltpu.make_async_remote_copy(
+            src_ref=leaving.at[g], dst_ref=coming.at[g],
+            send_sem=out_send.at[g], recv_sem=out_recv.at[g],
+            device_id={"tok": chip(g)}, device_id_type=MESH)
+
+    def row_block(q):
+        return pl.ds(pl.multiple_of(q * rows, 8), rows)
 
     def last_copy(step):
         return pltpu.make_async_remote_copy(
-            src_ref=leaving.at[(nx - 1) * nr + step], dst_ref=coming.at[(nx - 1) * nr + r],
-            send_sem=out_send.at[(nx - 1) * nr + step], recv_sem=out_recv.at[(nx - 1) * nr + r],
+            src_ref=leaving.at[nx - 1 + step], dst_ref=coming.at[nx - 1 + r],
+            send_sem=out_send.at[nx - 1 + step], recv_sem=out_recv.at[nx - 1 + r],
             device_id={"rep": lax.rem(r + step, nr)}, device_id_type=MESH)
 
     starts = HOP * jnp.minimum(z, nf - 1 - z) + nr * early - nr
@@ -288,15 +328,24 @@
 
             @pl.when(k == jnp.maximum(*ends))
             def _():
-                for q in range(nr):
-                    leaving[g * nr + q] = acc[g, q * rows:(q + 1) * rows, :].astype(jnp.bfloat16)
-                    out_copy(g, q).start()
-
-    for step in range(1, nr):
-        at = pl.ds(pl.multiple_of(lax.rem(r + step, nr) * rows, 8), rows)
-        leaving[(nx - 1) * nr + step] = acc[nx - 1, at, :].astype(jnp.bfloat16)
+                for step in range(1, nr):
+                    shared[g, step] = acc[g, row_block(lax.rem(r + step, nr)), :].astype(jnp.bfloat16)
+                    cross_copy(g, step).start()
+
+            @pl.when(k == jnp.maximum(*ends) + PAUSE)
+            def _():
+                total = acc[g, row_block(r), :]
+                for step in range(1, nr):
+                    q = lax.rem(r + step, nr)
+                    crossing(g, q).wait_recv()
+                    total += crossed[g, q].astype(jnp.float32)
+                leaving[g] = total.astype(jnp.bfloat16)
+                out_copy(g).start()
+
+    for step in range(1, nr):
+        leaving[nx - 1 + step] = acc[nx - 1, row_block(lax.rem(r + step, nr)), :].astype(jnp.bfloat16)
         last_copy(step).start()
-    final = acc[nx - 1, pl.ds(pl.multiple_of(r * rows, 8), rows), :]
+    final = acc[nx - 1, row_block(r), :]
 
     def summed(slot):
         pltpu.make_async_remote_copy(
@@ -305,10 +354,10 @@
             device_id={"rep": lax.rem(r + 1, nr)}, device_id_type=MESH).wait_recv()
         return coming[slot].astype(jnp.float32)
 
-    for slot in range((nx - 1) * nr):
-        final += summed(slot)
-    for step in range(1, nr):
-        final += summed((nx - 1) * nr + lax.rem(r + step, nr))
+    for g in range(nx - 1):
+        final += summed(nx - 2 - g)
+    for step in range(1, nr):
+        final += summed(nx - 1 + lax.rem(r + step, nr))
     out[...] = final.astype(out.dtype)
 
     for step in range(1, nr):
@@ -317,7 +366,9 @@
     for g in range(nx - 1):
         for q in range(nr):
             far_copy(g, q).wait_send()
-            out_copy(g, q).wait_send()
+        for step in range(1, nr):
+            cross_copy(g, step).wait_send()
+        out_copy(g).wait_send()
 
     @pl.loop(0, 2)
     def _(d):
@@ -350,7 +401,7 @@
         hbm, smem = pl.BlockSpec(memory_space=pl.ANY), pl.BlockSpec(memory_space=pltpu.SMEM)
         return pl.pallas_call(
             functools.partial(kernel, nf, nx, nr),
-            out_shape=jax.ShapeDtypeStruct((rows, feats), bf16),
+            out_shape=pltpu.VMEM((rows, feats), bf16),
             in_specs=[hbm] * 4 + [smem] * 3,
             out_specs=pl.BlockSpec(memory_space=pltpu.VMEM),
             scratch_shapes=[
@@ -363,12 +414,15 @@
                 pltpu.VMEM((2, units, nr, rows, 2 * width), bf16),
                 pltpu.VMEM((2, units, high, width), bf16),
                 pltpu.VMEM((nx, high, feats), f32),
-                pltpu.VMEM((nx * nr, rows, feats), bf16),
-                pltpu.VMEM((nx * nr, rows, feats), bf16),
+                pltpu.VMEM((nx - 1 + nr, rows, feats), bf16),
+                pltpu.VMEM((nx - 1 + nr, rows, feats), bf16),
+                pltpu.VMEM((max(nx - 1, 1), nr, rows, feats), bf16),
+                pltpu.VMEM((max(nx - 1, 1), nr, rows, feats), bf16),
                 dma((nx * nr,)), dma((nx * nr,)), dma(()),
                 dma((chunks,)), dma((chunks,)), dma((chunks,)),
                 dma((2, units, nr)), dma((2, units, nr)), dma((2, units)), dma((2, units)),
-                dma((nx * nr,)), dma((nx * nr,)),
+                dma((nx - 1 + nr,)), dma((nx - 1 + nr,)),
+                dma((max(nx - 1, 1), nr)), dma((max(nx - 1, 1), nr)),
             ],
             compiler_params=pltpu.CompilerParams(
                 collective_id=0, has_side_effects=True, vmem_limit_bytes=63 * 1024 * 1024),

time: 76.3 us -> 74.1 us (0.971)
  Pallas kernels: 74.4 us -> 73.2 us
  local copies, waits for them, and re-layouts: 1.64 us -> 0.69 us
    pallas_call x1, Pallas kernels: 74.4 us -> 73.2 us  [shards(): pl.pallas_call(functools.partial(kernel, nf, nx, nr), out_shape=pltpu.VME...]
    unnamed x1, local copies, waits for them, and re-layouts: 1.64 us -> 0.69 us
where the time goes in v2:
time: 74.1 us; the launch traced here: 73.9 us
  Pallas kernels  73.2 us (99%)
    pallas_call x1, Pallas kernels, shards(): pl.pallas_call(functools.partial(kernel, nf, nx, nr), out_shape=pltpu.VME...  73.2 us

profile of v2, /device:TPU:0, one launch (start us, length us, event | category | flops | bytes accessed | tf_op | source)
XLA Modules:
  0.0 73.9 jit_solution(10567228241887849288)
XLA Ops:
  0.0 73.2 %shard_map.73 = bf16[56,2048]{1,0:T(8,128)(2,1)S(1)} custom-call(bf16[56,2048]{1,0:T(8,128)(2,1)} %tokens.1, bf16[2048,3584]{1,0:T(8,128)(2,1)} %gate_w.1, bf16[2048,3584]{1,0:T(8,128)(2,1)} %up_w.1, bf16[3584,2048]{1,0:T(8,128)(2,1)} %down_w.1, s32[16,28]{1,0:T(8,128)} %gate_m.1, s32[16,28]{1,0:T(8,128)} %up_m.1, s32[16,28]{1,0:T(8,128)} %bitcast.1), custom_call_target="tpu_custom_call" | custom-call | tf_op jit(solution)/shard_map/pallas_call | solution.py:402
  73.3 0.7 copy.9

commit v3 on v2

--- a/solution.py
+++ b/solution.py
@@ -9,19 +9,20 @@
 
 BLOCK = 128
 HOP = 3
-BACK = 3
+BACK = 4
 LEAD = 2
-SLACK = 2
+SLACK = 1
 EARLY = 5
 HEADS = 2
 PAUSE = 2
+TAIL = 512
 MESH = pl.DeviceIdType.MESH
 
 
 def kernel(nf, nx, nr, tokens, gate_w, up_w, down_w, gate_m, up_m, down_m, out,
-           arrived, tok, wgu, wd, sums, part, taken, hid, acc, leaving, coming, shared, crossed,
+           arrived, tok, wgu, wd, sums, part, taken, hid, acc, leaving, coming, shared, crossed, ending, ended,
            tok_send, tok_recv, own_sem, g_sem, u_sem, d_sem, part_send, part_recv,
-           hid_send, hid_recv, out_send, out_recv, cross_send, cross_recv):
+           hid_send, hid_recv, out_send, out_recv, cross_send, cross_recv, end_send, end_recv):
     z, x, r = lax.axis_index("feat"), lax.axis_index("tok"), lax.axis_index("rep")
     rows = arrived.shape[1]
     feats = tok.shape[2]
@@ -29,6 +30,7 @@
     width = wd.shape[1]
     up_chunks, down_chunks = (chunks + 1) // 2, chunks // 2
     early = min(EARLY, down_chunks)
+    tail = TAIL if feats % TAIL == 0 else 2 * BLOCK
     peers = [(g, q) for g in range(nx) for q in range(nr)]
 
     def chip(g):
@@ -67,9 +69,15 @@
     lead = min(LEAD, down_chunks)
     for c in range(lead):
         for e in range(2):
+            near = jnp.minimum(z, nf - 1 - z)
+            p = near if e == 0 else nf - 1 - near
             j = jnp.where((z <= nf - 1 - z) == (e == 0), 0, up_chunks) + c
-            gate_copy(j).start(priority=1)
-            up_copy(j).start(priority=1)
+
+            @pl.when(nr * c + HOP * p < nr * lead)
+            def _():
+                gate_copy(j).start(priority=1)
+                up_copy(j).start(priority=1)
+
     acc[...] = jnp.zeros_like(acc)
 
     def splat(scalar, shape):
@@ -107,14 +115,21 @@
     own_copy.wait()
     side = (z > 0).astype(jnp.int32)
 
-    @pl.when((z == 0) | (z == nf - 1))
-    def _():
-        @pl.loop(0, heads)
-        def _(c):
+    def head(c):
+        @pl.when((z == 0) | (z == nf - 1))
+        def _():
             j = side * up_chunks + c
             gate_copy(j).wait()
             up_copy(j).wait()
             part[side, c, 0] = product(arrived[(nx - 1) * nr + r], j).astype(jnp.bfloat16)
+
+    def send_head(c):
+        @pl.when((z == 0) | (z == nf - 1))
+        def _():
+            part_copy(side, c, 0).start()
+
+    if heads:
+        head(0)
 
     ends = (z == 0).astype(jnp.int32) + (z == nf - 1).astype(jnp.int32)
     pl.semaphore_wait(barrier, nx * nr + 1 - ends)
@@ -138,17 +153,20 @@
             send_sem=tok_send.at[0], recv_sem=tok_recv.at[slot],
             device_id={"rep": lax.rem(r + 1, nr)}, device_id_type=MESH).wait_recv()
 
-    @pl.when((z == 0) | (z == nf - 1))
-    def _():
-        @pl.loop(0, heads)
-        def _(c):
-            part_copy(side, c, 0).start()
-
+    if heads:
+        send_head(0)
     for step in range(1, nr):
         near_copy(step).start()
     for g in range(nx - 1):
         for q in range(nr):
             far_copy(g, q).start()
+
+    if heads:
+        @pl.loop(1, heads)
+        def _(c):
+            head(c)
+            send_head(c)
+
     for step in range(1, nr):
         landed((nx - 1) * nr + lax.rem(r + step, nr))
     for q in range(nr):
@@ -181,6 +199,16 @@
     others = (nx - 1) * up_chunks
     begin = HOP * (nf - 1) + max(nr * (early + others) - others, (nr - 1) * nx * up_chunks) + SLACK
 
+    def prepare(k, d):
+        p, count, units = place(d)
+        t = k - HOP * p + nr + nr * lead
+        c = t // nr
+
+        @pl.when((t >= 0) & (c < count) & (t % nr == 0))
+        def _():
+            gate_copy(d * up_chunks + c).start(priority=1)
+            up_copy(d * up_chunks + c).start(priority=1)
+
     def multiply(k, d):
         p, count, units = place(d)
         t = k - HOP * p + nr
@@ -189,11 +217,6 @@
         @pl.when((t >= 0) & (u < units) & (t % nr == 0))
         def _():
             group, j, first = unit(u, d, count)
-
-            @pl.when(u + lead < count)
-            def _():
-                gate_copy(d * up_chunks + u + lead).start(priority=1)
-                up_copy(d * up_chunks + u + lead).start(priority=1)
 
             below = u - (count - lead if nx > 1 else 0)
 
@@ -238,38 +261,47 @@
                     gate, up = here[:, :width], here[:, width:]
                     hid[d, u, s * rows:(s + 1) * rows, :] = (gate / (1.0 + jnp.exp(-gate)) * up).astype(jnp.bfloat16)
 
+    def lower(d, u, group, j, n):
+        cols = slice(2 * n * BLOCK, 2 * (n + 1) * BLOCK)
+        tall = []
+        for b in range(width // BLOCK):
+            wide = []
+            for m in (2 * n, 2 * n + 1):
+                keep = down_m[m, j * (width // BLOCK) + b]
+                wide.append(wd[j, b * BLOCK:(b + 1) * BLOCK, m * BLOCK:(m + 1) * BLOCK] * splat(keep, (BLOCK, BLOCK)))
+            tall.append(jnp.concatenate(wide, axis=1))
+        acc[group, :, cols] += jnp.dot(hid[d, u], jnp.concatenate(tall, axis=0), preferred_element_type=jnp.float32)
+
+    def pass_on(h, d):
+        p, count, units = place(d)
+        u = hidden_unit(h, count)
+        group, j, _ = unit(u, d, count)
+
+        @pl.when(p < nf - 1)
+        def _():
+            hid_copy(d, u).wait_recv()
+
+        @pl.when(p > 0)
+        def _():
+            hid_copy(d, u).start()
+
+        @pl.when(h < count)
+        def _():
+            down_copy(j).wait()
+
+        return u, group, j
+
+    flip = (z > nf - 1 - z).astype(jnp.int32)
+
     def spread(k, d):
         p, count, units = place(d)
         h = k - begin - BACK * (nf - 1 - p)
 
-        @pl.when((h >= 0) & (h < units))
-        def _():
-            u = hidden_unit(h, count)
-            group, j, _ = unit(u, d, count)
-
-            @pl.when(p < nf - 1)
-            def _():
-                hid_copy(d, u).wait_recv()
-
-            @pl.when(p > 0)
-            def _():
-                hid_copy(d, u).start()
-
-            @pl.when(h < count)
-            def _():
-                down_copy(j).wait()
-
-            for n in range(wd.shape[2] // BLOCK // 2):
-                cols = slice(2 * n * BLOCK, 2 * (n + 1) * BLOCK)
-                tall = []
-                for b in range(width // BLOCK):
-                    wide = []
-                    for m in (2 * n, 2 * n + 1):
-                        keep = down_m[m, j * (width // BLOCK) + b]
-                        wide.append(wd[j, b * BLOCK:(b + 1) * BLOCK, m * BLOCK:(m + 1) * BLOCK] * splat(keep, (BLOCK, BLOCK)))
-                    tall.append(jnp.concatenate(wide, axis=1))
-                acc[group, :, cols] += jnp.dot(hid[d, u], jnp.concatenate(tall, axis=0),
-                                               preferred_element_type=jnp.float32)
+        @pl.when((h >= 0) & (h < units - (d == flip).astype(jnp.int32)))
+        def _():
+            u, group, j = pass_on(h, d)
+            for n in range(feats // (2 * BLOCK)):
+                lower(d, u, group, j, n)
 
     def cross_copy(g, step):
         return pltpu.make_async_remote_copy(
@@ -292,15 +324,21 @@
     def row_block(q):
         return pl.ds(pl.multiple_of(q * rows, 8), rows)
 
-    def last_copy(step):
-        return pltpu.make_async_remote_copy(
-            src_ref=leaving.at[nx - 1 + step], dst_ref=coming.at[nx - 1 + r],
-            send_sem=out_send.at[nx - 1 + step], recv_sem=out_recv.at[nx - 1 + r],
+    def last_copy(step, n):
+        cols = pl.ds(n * tail, tail)
+        return pltpu.make_async_remote_copy(
+            src_ref=ending.at[step, :, cols], dst_ref=ended.at[r, :, cols],
+            send_sem=end_send.at[step, n], recv_sem=end_recv.at[r, n],
             device_id={"rep": lax.rem(r + step, nr)}, device_id_type=MESH)
 
+    def last_landed(q, n):
+        cols = pl.ds(n * tail, tail)
+        pltpu.make_async_remote_copy(
+            src_ref=ending.at[0, :, cols], dst_ref=ended.at[q, :, cols],
+            send_sem=end_send.at[0, n], recv_sem=end_recv.at[q, n],
+            device_id={"rep": lax.rem(r + 1, nr)}, device_id_type=MESH).wait_recv()
+
     starts = HOP * jnp.minimum(z, nf - 1 - z) + nr * early - nr
-    flip = (z > nf - 1 - z).astype(jnp.int32)
-
     @pl.loop(-nr, begin + BACK * (nf - 1) + nx * up_chunks)
     def _(k):
         @pl.loop(0, 2)
@@ -316,6 +354,7 @@
 
         @pl.loop(0, 2)
         def _(e):
+            prepare(k, (e + flip) % 2)
             multiply(k, (e + flip) % 2)
 
         @pl.loop(0, 2)
@@ -342,27 +381,36 @@
                 leaving[g] = total.astype(jnp.bfloat16)
                 out_copy(g).start()
 
-    for step in range(1, nr):
-        leaving[nx - 1 + step] = acc[nx - 1, row_block(lax.rem(r + step, nr)), :].astype(jnp.bfloat16)
-        last_copy(step).start()
-    final = acc[nx - 1, row_block(r), :]
-
-    def summed(slot):
+    _, _, last_units = place(flip)
+    u, group, j = pass_on(last_units - 1, flip)
+    for n in range(feats // tail):
+        for b in range(tail // (2 * BLOCK)):
+            lower(flip, u, nx - 1, j, n * (tail // (2 * BLOCK)) + b)
+        cols = slice(n * tail, (n + 1) * tail)
+        for step in range(1, nr):
+            ending[step, :, cols] = acc[nx - 1, row_block(lax.rem(r + step, nr)), cols].astype(jnp.bfloat16)
+            last_copy(step, n).start()
+
+    own = row_block(r)
+    for g in range(nx - 1):
         pltpu.make_async_remote_copy(
-            src_ref=leaving.at[0], dst_ref=coming.at[slot],
-            send_sem=out_send.at[0], recv_sem=out_recv.at[slot],
+            src_ref=leaving.at[0], dst_ref=coming.at[g],
+            send_sem=out_send.at[0], recv_sem=out_recv.at[g],
             device_id={"rep": lax.rem(r + 1, nr)}, device_id_type=MESH).wait_recv()
-        return coming[slot].astype(jnp.float32)
-
-    for g in range(nx - 1):
-        final += summed(nx - 2 - g)
-    for step in range(1, nr):
-        final += summed(nx - 1 + lax.rem(r + step, nr))
-    out[...] = final.astype(out.dtype)
+        acc[nx - 1, own, :] += coming[g].astype(jnp.float32)
+    for n in range(feats // tail):
+        cols = slice(n * tail, (n + 1) * tail)
+        final = acc[nx - 1, own, cols]
+        for step in range(1, nr):
+            q = lax.rem(r + step, nr)
+            last_landed(q, n)
+            final += ended[q, :, cols].astype(jnp.float32)
+        out[:, cols] = final.astype(out.dtype)
 
     for step in range(1, nr):
         near_copy(step).wait_send()
-        last_copy(step).wait_send()
+        for n in range(feats // tail):
+            last_copy(step, n).wait_send()
     for g in range(nx - 1):
         for q in range(nr):
             far_copy(g, q).wait_send()
@@ -396,6 +444,7 @@
         chunks = hidden // width
         units = nx * ((chunks + 1) // 2)
         high = nr * rows
+        pieces = feats // (TAIL if feats % TAIL == 0 else 2 * BLOCK)
         bf16, f32 = jnp.bfloat16, jnp.float32
         dma = pltpu.SemaphoreType.DMA
         hbm, smem = pl.BlockSpec(memory_space=pl.ANY), pl.BlockSpec(memory_space=pltpu.SMEM)
@@ -414,15 +463,18 @@
                 pltpu.VMEM((2, units, nr, rows, 2 * width), bf16),
                 pltpu.VMEM((2, units, high, width), bf16),
                 pltpu.VMEM((nx, high, feats), f32),
-                pltpu.VMEM((nx - 1 + nr, rows, feats), bf16),
-                pltpu.VMEM((nx - 1 + nr, rows, feats), bf16),
+                pltpu.VMEM((max(nx - 1, 1), rows, feats), bf16),
+                pltpu.VMEM((max(nx - 1, 1), rows, feats), bf16),
                 pltpu.VMEM((max(nx - 1, 1), nr, rows, feats), bf16),
                 pltpu.VMEM((max(nx - 1, 1), nr, rows, feats), bf16),
+                pltpu.VMEM((nr, rows, feats), bf16),
+                pltpu.VMEM((nr, rows, feats), bf16),
                 dma((nx * nr,)), dma((nx * nr,)), dma(()),
                 dma((chunks,)), dma((chunks,)), dma((chunks,)),
                 dma((2, units, nr)), dma((2, units, nr)), dma((2, units)), dma((2, units)),
-                dma((nx - 1 + nr,)), dma((nx - 1 + nr,)),
+                dma((max(nx - 1, 1),)), dma((max(nx - 1, 1),)),
                 dma((max(nx - 1, 1), nr)), dma((max(nx - 1, 1), nr)),
+                dma((nr, pieces)), dma((nr, pieces)),
             ],
             compiler_params=pltpu.CompilerParams(
                 collective_id=0, has_side_effects=True, vmem_limit_bytes=63 * 1024 * 1024),

time: 74.1 us -> 72.9 us (0.984)
  Pallas kernels: 73.2 us -> 72 us
    pallas_call x1, Pallas kernels: 73.2 us -> 72 us  [shards(): pl.pallas_call(functools.partial(kernel, nf, nx, nr), out_shape=pltpu.VME...]
where the time goes in v3:
time: 72.9 us; the launch traced here: 72.7 us
  Pallas kernels  72 us (99%)
    pallas_call x1, Pallas kernels, shards(): pl.pallas_call(functools.partial(kernel, nf, nx, nr), out_shape=pltpu.VME...  72 us

profile of v3, /device:TPU:0, one launch (start us, length us, event | category | flops | bytes accessed | tf_op | source)
XLA Modules:
  0.0 72.7 jit_solution(10255042703038525349)
XLA Ops:
  0.0 72.0 %shard_map.73 = bf16[56,2048]{1,0:T(8,128)(2,1)S(1)} custom-call(bf16[56,2048]{1,0:T(8,128)(2,1)} %tokens.1, bf16[2048,3584]{1,0:T(8,128)(2,1)} %gate_w.1, bf16[2048,3584]{1,0:T(8,128)(2,1)} %up_w.1, bf16[3584,2048]{1,0:T(8,128)(2,1)} %down_w.1, s32[16,28]{1,0:T(8,128)} %gate_m.1, s32[16,28]{1,0:T(8,128)} %up_m.1, s32[16,28]{1,0:T(8,128)} %bitcast.1), custom_call_target="tpu_custom_call" | custom-call | tf_op jit(solution)/shard_map/pallas_call | solution.py:451
  72.0 0.7 copy.9

commit v4 on v3

--- a/solution.py
+++ b/solution.py
@@ -19,10 +19,10 @@
 MESH = pl.DeviceIdType.MESH
 
 
-def kernel(nf, nx, nr, tokens, gate_w, up_w, down_w, gate_m, up_m, down_m, out,
-           arrived, tok, wgu, wd, sums, part, taken, hid, acc, leaving, coming, shared, crossed, ending, ended,
+def kernel(nf, nx, nr, tokens, gate_w, up_w, down_w, gate_b, up_b, down_b, out,
+           arrived, tok, wgu, wd, sums, part, taken, hid, acc, leaving, coming, shared, crossed, ending, ended, gate_m, up_m, down_m,
            tok_send, tok_recv, own_sem, g_sem, u_sem, d_sem, part_send, part_recv,
-           hid_send, hid_recv, out_send, out_recv, cross_send, cross_recv, end_send, end_recv):
+           hid_send, hid_recv, out_send, out_recv, cross_send, cross_recv, end_send, end_recv, mask_sem):
     z, x, r = lax.axis_index("feat"), lax.axis_index("tok"), lax.axis_index("rep")
     rows = arrived.shape[1]
     feats = tok.shape[2]
@@ -64,6 +64,10 @@
         return pltpu.make_async_copy(down_w.at[at, :], wd.at[j], d_sem.at[j])
 
     own_copy = pltpu.make_async_copy(tokens, arrived.at[(nx - 1) * nr + r], own_sem)
+    mask_copies = [pltpu.make_async_copy(src, dst, mask_sem.at[i])
+                   for i, (src, dst) in enumerate(((gate_b, gate_m), (up_b, up_m), (down_b, down_m)))]
+    for copy in mask_copies:
+        copy.start()
     own_copy.start()
 
     lead = min(LEAD, down_chunks)
@@ -113,6 +117,8 @@
 
     heads = min(HEADS, down_chunks, early) if nr == 2 and nf > 1 else 0
     own_copy.wait()
+    for copy in mask_copies:
+        copy.wait()
     side = (z > 0).astype(jnp.int32)
 
     def head(c):
@@ -447,11 +453,11 @@
         pieces = feats // (TAIL if feats % TAIL == 0 else 2 * BLOCK)
         bf16, f32 = jnp.bfloat16, jnp.float32
         dma = pltpu.SemaphoreType.DMA
-        hbm, smem = pl.BlockSpec(memory_space=pl.ANY), pl.BlockSpec(memory_space=pltpu.SMEM)
+        hbm = pl.BlockSpec(memory_space=pl.ANY)
         return pl.pallas_call(
             functools.partial(kernel, nf, nx, nr),
             out_shape=pltpu.VMEM((rows, feats), bf16),
-            in_specs=[hbm] * 4 + [smem] * 3,
+            in_specs=[hbm] * 7,
             out_specs=pl.BlockSpec(memory_space=pltpu.VMEM),
             scratch_shapes=[
                 pltpu.VMEM((nx * nr, rows, feats), bf16),
@@ -469,12 +475,14 @@
                 pltpu.VMEM((max(nx - 1, 1), nr, rows, feats), bf16),
                 pltpu.VMEM((nr, rows, feats), bf16),
                 pltpu.VMEM((nr, rows, feats), bf16),
+                pltpu.SMEM(gate_mask.shape, jnp.int32), pltpu.SMEM(up_mask.shape, jnp.int32),
+                pltpu.SMEM(down_mask.shape[::-1], jnp.int32),
                 dma((nx * nr,)), dma((nx * nr,)), dma(()),
                 dma((chunks,)), dma((chunks,)), dma((chunks,)),
                 dma((2, units, nr)), dma((2, units, nr)), dma((2, units)), dma((2, units)),
                 dma((max(nx - 1, 1),)), dma((max(nx - 1, 1),)),
                 dma((max(nx - 1, 1), nr)), dma((max(nx - 1, 1), nr)),
-                dma((nr, pieces)), dma((nr, pieces)),
+                dma((nr, pieces)), dma((nr, pieces)), dma((3,)),
             ],
             compiler_params=pltpu.CompilerParams(
                 collective_id=0, has_side_effects=True, vmem_limit_bytes=63 * 1024 * 1024),

time: 72.9 us -> 71.8 us (0.985)
  Pallas kernels: 72 us -> 70.9 us
    pallas_call x1, Pallas kernels: 72 us -> 70.9 us  [shards(): pl.pallas_call(functools.partial(kernel, nf, nx, nr), out_shape=pltpu.VME...]
where the time goes in v4:
time: 71.8 us; the launch traced here: 71.6 us
  Pallas kernels  70.9 us (99%)
    pallas_call x1, Pallas kernels, shards(): pl.pallas_call(functools.partial(kernel, nf, nx, nr), out_shape=pltpu.VME...  70.9 us

profile of v4, /device:TPU:0, one launch (start us, length us, event | category | flops | bytes accessed | tf_op | source)
XLA Modules:
  0.0 71.6 jit_solution(794557421323085718)
XLA Ops:
  0.0 70.9 %shard_map.73 = bf16[56,2048]{1,0:T(8,128)(2,1)S(1)} custom-call(bf16[56,2048]{1,0:T(8,128)(2,1)} %tokens.1, bf16[2048,3584]{1,0:T(8,128)(2,1)} %gate_w.1, bf16[2048,3584]{1,0:T(8,128)(2,1)} %up_w.1, bf16[3584,2048]{1,0:T(8,128)(2,1)} %down_w.1, s32[16,28]{1,0:T(8,128)} %gate_b.1, s32[16,28]{1,0:T(8,128)} %up_b.1, s32[16,28]{1,0:T(8,128)} %bitcast.1), custom_call_target="tpu_custom_call" | custom-call | tf_op jit(solution)/shard_map/pallas_call | solution.py:457
  70.9 0.7 copy.9

commit v5 on v4

--- a/solution.py
+++ b/solution.py
@@ -397,6 +397,30 @@
             ending[step, :, cols] = acc[nx - 1, row_block(lax.rem(r + step, nr)), cols].astype(jnp.bfloat16)
             last_copy(step, n).start()
 
+    for step in range(1, nr):
+        near_copy(step).wait_send()
+    for g in range(nx - 1):
+        for q in range(nr):
+            far_copy(g, q).wait_send()
+        for step in range(1, nr):
+            cross_copy(g, step).wait_send()
+        out_copy(g).wait_send()
+
+    @pl.loop(0, 2)
+    def _(d):
+        p, count, units = place(d)
+
+        @pl.loop(0, nx * up_chunks)
+        def _(u):
+            @pl.when((u < units) & (p < nf - 1))
+            def _():
+                for m in range(nr):
+                    part_copy(d, u, m).wait_send()
+
+            @pl.when((u < units) & (p > 0))
+            def _():
+                hid_copy(d, u).wait_send()
+
     own = row_block(r)
     for g in range(nx - 1):
         pltpu.make_async_remote_copy(
@@ -414,30 +438,8 @@
         out[:, cols] = final.astype(out.dtype)
 
     for step in range(1, nr):
-        near_copy(step).wait_send()
         for n in range(feats // tail):
             last_copy(step, n).wait_send()
-    for g in range(nx - 1):
-        for q in range(nr):
-            far_copy(g, q).wait_send()
-        for step in range(1, nr):
-            cross_copy(g, step).wait_send()
-        out_copy(g).wait_send()
-
-    @pl.loop(0, 2)
-    def _(d):
-        p, count, units = place(d)
-
-        @pl.loop(0, nx * up_chunks)
-        def _(u):
-            @pl.when((u < units) & (p < nf - 1))
-            def _():
-                for m in range(nr):
-                    part_copy(d, u, m).wait_send()
-
-            @pl.when((u < units) & (p > 0))
-            def _():
-                hid_copy(d, u).wait_send()
 
 
 def solution(mesh):

time: 71.8 us -> 71.4 us (level)
  no operation moved by 1% of the time
where the time goes in v5:
time: 71.4 us; the launch traced here: 71.3 us
  Pallas kernels  70.6 us (99%)
    pallas_call x1, Pallas kernels, shards(): pl.pallas_call(functools.partial(kernel, nf, nx, nr), out_shape=pltpu.VME...  70.6 us

profile of v5, /device:TPU:0, one launch (start us, length us, event | category | flops | bytes accessed | tf_op | source)
XLA Modules:
  0.0 71.3 jit_solution(904873640800618355)
XLA Ops:
  0.0 70.6 %shard_map.73 = bf16[56,2048]{1,0:T(8,128)(2,1)S(1)} custom-call(bf16[56,2048]{1,0:T(8,128)(2,1)} %tokens.1, bf16[2048,3584]{1,0:T(8,128)(2,1)} %gate_w.1, bf16[2048,3584]{1,0:T(8,128)(2,1)} %up_w.1, bf16[3584,2048]{1,0:T(8,128)(2,1)} %down_w.1, s32[16,28]{1,0:T(8,128)} %gate_b.1, s32[16,28]{1,0:T(8,128)} %up_b.1, s32[16,28]{1,0:T(8,128)} %bitcast.1), custom_call_target="tpu_custom_call" | custom-call | tf_op jit(solution)/shard_map/pallas_call | solution.py:459
  70.6 0.7 copy.9

commit v6 on v5

--- a/solution.py
+++ b/solution.py
@@ -387,6 +387,23 @@
                 leaving[g] = total.astype(jnp.bfloat16)
                 out_copy(g).start()
 
+    for step in range(1, nr):
+        near_copy(step).wait_send()
+    for g in range(nx - 1):
+        for q in range(nr):
+            far_copy(g, q).wait_send()
+
+    @pl.loop(0, 2)
+    def _(d):
+        p, count, units = place(d)
+
+        @pl.loop(0, nx * up_chunks)
+        def _(u):
+            @pl.when((u < units) & (p < nf - 1))
+            def _():
+                for m in range(nr):
+                    part_copy(d, u, m).wait_send()
+
     _, _, last_units = place(flip)
     u, group, j = pass_on(last_units - 1, flip)
     for n in range(feats // tail):
@@ -397,11 +414,7 @@
             ending[step, :, cols] = acc[nx - 1, row_block(lax.rem(r + step, nr)), cols].astype(jnp.bfloat16)
             last_copy(step, n).start()
 
-    for step in range(1, nr):
-        near_copy(step).wait_send()
     for g in range(nx - 1):
-        for q in range(nr):
-            far_copy(g, q).wait_send()
         for step in range(1, nr):
             cross_copy(g, step).wait_send()
         out_copy(g).wait_send()
@@ -412,11 +425,6 @@
 
         @pl.loop(0, nx * up_chunks)
         def _(u):
-            @pl.when((u < units) & (p < nf - 1))
-            def _():
-                for m in range(nr):
-                    part_copy(d, u, m).wait_send()
-
             @pl.when((u < units) & (p > 0))
             def _():
                 hid_copy(d, u).wait_send()

time: 71.4 us -> 71.7 us (level)
  no operation moved by 1% of the time
where the time goes in v6:
time: 71.7 us; the launch traced here: 71.5 us
  Pallas kernels  70.8 us (99%)
    pallas_call x1, Pallas kernels, shards(): pl.pallas_call(functools.partial(kernel, nf, nx, nr), out_shape=pltpu.VME...  70.8 us

profile of v6, /device:TPU:0, one launch (start us, length us, event | category | flops | bytes accessed | tf_op | source)
XLA Modules:
  0.0 71.5 jit_solution(427826951984300711)
XLA Ops:
  0.0 70.8 %shard_map.73 = bf16[56,2048]{1,0:T(8,128)(2,1)S(1)} custom-call(bf16[56,2048]{1,0:T(8,128)(2,1)} %tokens.1, bf16[2048,3584]{1,0:T(8,128)(2,1)} %gate_w.1, bf16[2048,3584]{1,0:T(8,128)(2,1)} %up_w.1, bf16[3584,2048]{1,0:T(8,128)(2,1)} %down_w.1, s32[16,28]{1,0:T(8,128)} %gate_b.1, s32[16,28]{1,0:T(8,128)} %up_b.1, s32[16,28]{1,0:T(8,128)} %bitcast.1), custom_call_target="tpu_custom_call" | custom-call | tf_op jit(solution)/shard_map/pallas_call | solution.py:467
  70.8 0.7 copy.9
